TPU v7x, 32 devices: a whole 2x2x4 slice. The times are simulated.
32 devices in a mesh: dp: 4 (over y, x), expert: 8 (over z, core).
Axes of the slice: x: 2, y: 2, z: 4, core: 2. Of those that a mesh axis runs over, the one named last changes fastest.
Arguments:
- tokens: bfloat16 [1024, 1024], P(('dp', 'expert')), may hold values from -6 to 6
- cotangent: bfloat16 [1024, 1024], P(('dp', 'expert')), may hold values from -3 to 3
- routes: int32 [1024, 8], P(('dp', 'expert')), may hold values from 0 to 7, as said below
- combine: bfloat16 [1024, 8], P(('dp', 'expert')), may hold values from 0.099609375 to 1
- hot_experts: int32 [4], replicated, may hold values from 0 to 3, as said below
- extra_slots: int32 [4], replicated, may hold values from 1 to 4, as said below
- w_gate: bfloat16 [8, 1024, 384], P('expert'), may hold values from -0.1875 to 0.1875
- w_up: bfloat16 [8, 1024, 384], P('expert'), may hold values from -0.1875 to 0.1875
- w_down: bfloat16 [8, 384, 1024], P('expert'), may hold values from -0.3125 to 0.3125
Outputs:
- token_grads: bfloat16 [1024, 1024], P(('dp', 'expert'))
- grad_gate: bfloat16 [8, 1024, 384], P('expert', 'dp')
- grad_up: bfloat16 [8, 1024, 384], P('expert', 'dp')
- grad_down: bfloat16 [8, 384, 1024], P('expert')
Inputs may be any that keep to these rules, and one draw needn't show every extreme that they name: `routes`: each row names 8 different experts. `hot_experts`: 4 different experts, all below 4. `extra_slots`: one of the entries equals 4.
All inputs are finite; a program needn't handle non-finite values.
Results may differ from a plain program's by a relative error of at most 0.0064.
Values may be sent and summed in bfloat16 or wider, within the bound.
A program may use at most 64 MiB of HBM per device.

v0:
```python
import jax
import jax.numpy as jnp
from jax import lax
from jax.sharding import PartitionSpec as P


def forward_rows(weight_gate, weight_up, weight_down, row_tokens, row_cotan, row_weights):
    gate_pre = jnp.dot(row_tokens, weight_gate, preferred_element_type=jnp.float32)
    up_proj = jnp.dot(row_tokens, weight_up, preferred_element_type=jnp.float32)
    sigmoid_gate = jax.nn.sigmoid(gate_pre)
    gate_act = gate_pre * sigmoid_gate
    hidden = (gate_act * up_proj).astype(jnp.bfloat16)
    out_grad = (row_weights.astype(jnp.float32)[:, None] * row_cotan.astype(jnp.float32)).astype(
        jnp.bfloat16
    )
    hidden_grad = jnp.dot(out_grad, weight_down.T, preferred_element_type=jnp.float32)
    gate_grad = (
        hidden_grad * up_proj * sigmoid_gate * (1.0 + gate_pre * (1.0 - sigmoid_gate))
    ).astype(jnp.bfloat16)
    up_grad = (hidden_grad * gate_act).astype(jnp.bfloat16)
    row_grads = jnp.dot(gate_grad, weight_gate.T, preferred_element_type=jnp.float32)
    row_grads = row_grads + jnp.dot(up_grad, weight_up.T, preferred_element_type=jnp.float32)
    return (row_grads.astype(jnp.bfloat16), (row_tokens, gate_grad, up_grad, hidden, out_grad))


def weight_terms(pieces):
    row_tokens, gate_grad, up_grad, hidden, out_grad = pieces
    grad_gate = jnp.dot(row_tokens.T, gate_grad, preferred_element_type=jnp.float32)
    grad_up = jnp.dot(row_tokens.T, up_grad, preferred_element_type=jnp.float32)
    grad_down = jnp.dot(hidden.T, out_grad, preferred_element_type=jnp.float32)
    return (grad_gate, grad_up, grad_down)


def expert_pass(weight_gate, weight_up, weight_down, row_tokens, row_cotan, row_weights):
    row_grads, pieces = forward_rows(
        weight_gate, weight_up, weight_down, row_tokens, row_cotan, row_weights
    )
    return (row_grads, weight_terms(pieces))


def shards(tokens, cotangent, routes, combine, hot_experts, extra_slots, w_gate, w_up, w_down):
    expert_count = lax.axis_size("expert")
    token_count, features = tokens.shape
    route_count = routes.shape[1]
    capacity = max(2, min(token_count * route_count * 7 // (8 * expert_count), token_count // 2))
    spare_slots = 2 * max(1, capacity // 6)
    expert_ids = routes.reshape(-1)
    assign_count = expert_ids.shape[0]
    assign_order = jnp.arange(assign_count, dtype=jnp.int32)
    earlier = (expert_ids[:, None] == expert_ids[None, :]) & (
        assign_order[None, :] < assign_order[:, None]
    )
    slot_rank = jnp.sum(earlier.astype(jnp.int32), axis=1)
    hot_match = expert_ids[:, None] == hot_experts[None, :]
    slot_limit = capacity + jnp.sum(jnp.where(hot_match, extra_slots[None, :], 0), axis=1)
    is_kept = slot_rank < slot_limit
    slot_count = capacity + spare_slots
    total_slots = expert_count * slot_count
    flat_slot = jnp.where(is_kept, expert_ids * slot_count + slot_rank, total_slots)
    slot_ids = jnp.arange(total_slots, dtype=jnp.int32)
    assign_onehot = slot_ids[:, None] == flat_slot[None, :]
    token_onehot = jnp.any(
        assign_onehot.reshape(total_slots, token_count, route_count), axis=2
    ).astype(jnp.bfloat16)
    both_rows = jnp.concatenate([tokens, cotangent], axis=1)
    filled = jnp.dot(token_onehot, both_rows, preferred_element_type=jnp.float32).astype(
        jnp.bfloat16
    )
    token_send = filled[:, :features].reshape(expert_count, slot_count, features)
    cotan_send = filled[:, features:].reshape(expert_count, slot_count, features)
    weight_flat = jnp.sum(
        jnp.where(assign_onehot, combine.reshape(-1).astype(jnp.float32)[None, :], 0.0), axis=1
    )
    weight_send = weight_flat.astype(jnp.bfloat16).reshape(expert_count, slot_count)
    token_recv, cotan_recv, weight_recv = (
        lax.all_to_all(token_send, "expert", split_axis=0, concat_axis=0, tiled=True),
        lax.all_to_all(cotan_send, "expert", split_axis=0, concat_axis=0, tiled=True),
        lax.all_to_all(weight_send, "expert", split_axis=0, concat_axis=0, tiled=True),
    )
    own_weights = (w_gate[0], w_up[0], w_down[0])
    all_rows, grad_terms = expert_pass(
        own_weights[0],
        own_weights[1],
        own_weights[2],
        token_recv.reshape(-1, features),
        cotan_recv.reshape(-1, features),
        weight_recv.reshape(-1),
    )
    grad_rows = all_rows.reshape(expert_count, slot_count, features)
    returned_rows = lax.all_to_all(grad_rows, "expert", split_axis=0, concat_axis=0, tiled=True)
    token_grads = jnp.dot(
        token_onehot.T,
        returned_rows.reshape(total_slots, features),
        preferred_element_type=jnp.float32,
    ).astype(jnp.bfloat16)
    grad_gate, grad_up = (
        lax.psum_scatter(grad_terms[0][None], "dp", scatter_dimension=1, tiled=True),
        lax.psum_scatter(grad_terms[1][None], "dp", scatter_dimension=1, tiled=True),
    )
    grad_down = lax.psum(grad_terms[2][None], "dp")
    return (
        token_grads,
        grad_gate.astype(jnp.bfloat16),
        grad_up.astype(jnp.bfloat16),
        grad_down.astype(jnp.bfloat16),
    )


def solution(mesh):
    in_specs = (
        P(("dp", "expert"), None),
        P(("dp", "expert"), None),
        P(("dp", "expert"), None),
        P(("dp", "expert"), None),
        P(),
        P(),
        P("expert", None, None),
        P("expert", None, None),
        P("expert", None, None),
    )
    out_specs = (
        P(("dp", "expert"), None),
        P("expert", "dp", None),
        P("expert", "dp", None),
        P("expert", None, None),
    )
    return jax.shard_map(shards, mesh=mesh, in_specs=in_specs, out_specs=out_specs, check_vma=False)
```

profile of v0, /device:TPU:0, one launch (start us, length us, event | category | flops | bytes accessed | tf_op | source)
XLA Modules:
  0.0 155.9 jit_solution(16793875699837294183)
XLA Ops:
  7.2 0.0 copy-start
  7.2 0.8 copy.24
  8.0 0.1 eq.49
  8.1 0.2 convert_reduce_fusion
  8.3 0.8 copy.26
  9.1 0.1 reshape.103
  9.1 0.8 select_reduce_fusion.1
  9.9 0.1 select_reduce_fusion
  10.0 0.7 convert_element_type.116
  10.7 6.4 %all-to-all-start = ((bf16[8,1,20]{2,1,0:T(2,128)(2,1)}), bf16[8,1,20]{2,1,0:T(2,128)(2,1)S(1)}, u32[]{:S(2)}, u32[]{:S(2)}) async-start(bf16[8,1,20]{2,1,0:T(2,128)(2,1)} %convert_element_type.116), calls=%async_computation | async-start | bytes 8192 | tf_op jit(solution)/shard_map/all_to_all | solution.py:78
  17.1 0.1 reduce_sum.30
  17.2 0.1 add.41
  17.3 0.2 fusion.11
  17.4 1.2 convolution_convert_fusion
  18.7 0.8 reshape.99
  19.5 3.0 %all-to-all-done = bf16[8,1,20]{2,1,0:T(2,128)(2,1)S(1)} async-done(((bf16[8,1,20]{2,1,0:T(2,128)(2,1)}), bf16[8,1,20]{2,1,0:T(2,128)(2,1)S(1)}, u32[]{:S(2)}, u32[]{:S(2)}) %all-to-all-start) | async-done | bytes 352 | tf_op jit(solution)/shard_map/all_to_all | solution.py:78
  22.6 3.5 %all-to-all-start.2 = ((bf16[8,20,1024]{2,1,0:T(8,128)(2,1)}), bf16[8,20,1024]{2,1,0:T(8,128)(2,1)S(1)}, u32[]{:S(2)}, u32[]{:S(2)}) async-start(bf16[8,20,1024]{2,1,0:T(8,128)(2,1)} %reshape.99), calls=%async_computation.2 | async-start | bytes 786432 | tf_op jit(solution)/shard_map/all_to_all | solution.py:76
  26.1 0.8 reshape.98
  26.9 0.0 copy-start.1
  26.9 11.6 %all-to-all-done.2 = bf16[8,20,1024]{2,1,0:T(8,128)(2,1)S(1)} async-done(((bf16[8,20,1024]{2,1,0:T(8,128)(2,1)}), bf16[8,20,1024]{2,1,0:T(8,128)(2,1)S(1)}, u32[]{:S(2)}, u32[]{:S(2)}) %all-to-all-start.2) | async-done | bytes 327712 | tf_op jit(solution)/shard_map/all_to_all | solution.py:76
  38.5 3.5 %all-to-all-start.1 = ((bf16[8,20,1024]{2,1,0:T(8,128)(2,1)}), bf16[8,20,1024]{2,1,0:T(8,128)(2,1)S(1)}, u32[]{:S(2)}, u32[]{:S(2)}) async-start(bf16[8,20,1024]{2,1,0:T(8,128)(2,1)} %reshape.98), calls=%async_computation.1 | async-start | bytes 786432 | tf_op jit(solution)/shard_map/all_to_all | solution.py:77
  42.0 0.0 reduce-scatter.3.cloned.1.call-start
  42.0 0.1 reshape.100
  42.1 0.0 copy-done
  42.1 0.3 fusion.3
  42.4 0.0 copy-done.1
  42.5 0.0 copy-start.2
  42.5 0.3 fusion.6
  42.8 0.0 copy-start.3
  42.8 11.6 %all-to-all-done.1 = bf16[8,20,1024]{2,1,0:T(8,128)(2,1)S(1)} async-done(((bf16[8,20,1024]{2,1,0:T(8,128)(2,1)}), bf16[8,20,1024]{2,1,0:T(8,128)(2,1)S(1)}, u32[]{:S(2)}, u32[]{:S(2)}) %all-to-all-start.1) | async-done | bytes 327712 | tf_op jit(solution)/shard_map/all_to_all | solution.py:77
  54.4 0.1 multiply_convert_fusion
  54.5 0.1 convert_element_type.98
  54.6 1.6 multiply_convert_fusion.4
  56.2 1.6 %convolution_bitcast_fusion.2 = f32[1,1024,384]{2,1,0:T(8,128)} fusion(bf16[160,1024]{1,0:T(8,128)(2,1)S(1)} %reshape.100, bf16[160,384]{1,0:T(8,128)(2,1)S(1)} %get-tuple-element.7), kind=kOutput, calls=%fused_computation.3 | convolution fusion | flops 125829120 | bytes 2023424 | tf_op jit(solution)/shard_map/dot_general | solution.py:28
  57.8 0.0 reduce-scatter.3.cloned.1.call-update
  57.8 0.0 reduce-scatter.5.cloned.1.call-start
  57.9 1.6 %convolution_bitcast_fusion.1 = f32[1,1024,384]{2,1,0:T(8,128)} fusion(bf16[160,1024]{1,0:T(8,128)(2,1)S(1)} %reshape.100, bf16[160,384]{1,0:T(8,128)(2,1)S(1)} %get-tuple-element.6), kind=kOutput, calls=%fused_computation.2 | convolution fusion | flops 125829120 | bytes 2023424 | tf_op jit(solution)/shard_map/dot_general | solution.py:29
  59.5 0.0 copy-done.2
  59.5 0.0 copy-done.3
  59.5 0.0 reduce-scatter.5.cloned.1.call-update
  59.6 0.1 reshape.105
  59.6 0.4 fusion.1
  60.1 0.4 fusion
  60.5 0.8 reshape.101
  61.3 3.5 %all-to-all-start.3 = ((bf16[8,20,1024]{2,1,0:T(8,128)(2,1)}), bf16[8,20,1024]{2,1,0:T(8,128)(2,1)S(1)}, u32[]{:S(2)}, u32[]{:S(2)}) async-start(bf16[8,20,1024]{2,1,0:T(8,128)(2,1)} %reshape.101), calls=%async_computation.3 | async-start | bytes 786432 | tf_op jit(solution)/shard_map/all_to_all | solution.py:90
  64.7 0.1 reshape.106
  64.8 1.5 convolution_bitcast_fusion
  66.3 78.5 %all-reduce.1 = bf16[1,384,1024]{2,1,0:T(8,128)(2,1)} all-reduce(f32[1,384,1024]{2,1,0:T(8,128)S(1)} %convolution_bitcast_fusion), channel_id=1, replica_groups=mesh['dp'=4,'expert'=8] {'dp'}, use_global_device_ids=true, to_apply=%region_6.7 | all-reduce | flops 393216 | bytes 2359296 | tf_op jit(solution)/shard_map/psum | solution.py:100
  144.8 0.0 all-to-all-done.3
  144.8 0.1 reshape.102
  144.9 0.8 convolution_convert_fusion.1
  145.7 0.0 reduce-scatter.3.cloned.1.call-done
  145.7 1.7 %convert_element_type.103 = bf16[1,256,384]{2,1,0:T(8,128)(2,1)} convert(f32[1,256,384]{2,1,0:T(8,128)} %reduce-scatter.3.cloned.1.call-done) | non-fusion elementwise | flops 98304 | bytes 589824 | tf_op jit(solution)/shard_map/convert_element_type | solution.py:103
  147.4 0.0 reduce-scatter.5.cloned.1.call-done
  147.4 1.7 %convert_element_type.104 = bf16[1,256,384]{2,1,0:T(8,128)(2,1)} convert(f32[1,256,384]{2,1,0:T(8,128)} %reduce-scatter.5.cloned.1.call-done) | non-fusion elementwise | flops 98304 | bytes 589824 | tf_op jit(solution)/shard_map/convert_element_type | solution.py:104
  (5 shorter events, 0.1 us)
Async XLA Ops:
  7.2 34.9 %copy-start = (bf16[1,1024,384]{2,1,0:T(8,128)(2,1)S(1)}, bf16[1,1024,384]{2,1,0:T(8,128)(2,1)}, u32[]{:S(2)}) copy-start(bf16[1,1024,384]{2,1,0:T(8,128)(2,1)} %param.15) | copy-start | bytes 2359300
  10.7 11.9 %all-to-all-start = ((bf16[8,1,20]{2,1,0:T(2,128)(2,1)}), bf16[8,1,20]{2,1,0:T(2,128)(2,1)S(1)}, u32[]{:S(2)}, u32[]{:S(2)}) async-start(bf16[8,1,20]{2,1,0:T(2,128)(2,1)} %convert_element_type.116), calls=%async_computation | async-start | bytes 8192 | tf_op jit(solution)/shard_map/all_to_all | solution.py:78
  22.6 15.9 %all-to-all-start.2 = ((bf16[8,20,1024]{2,1,0:T(8,128)(2,1)}), bf16[8,20,1024]{2,1,0:T(8,128)(2,1)S(1)}, u32[]{:S(2)}, u32[]{:S(2)}) async-start(bf16[8,20,1024]{2,1,0:T(8,128)(2,1)} %reshape.99), calls=%async_computation.2 | async-start | bytes 786432 | tf_op jit(solution)/shard_map/all_to_all | solution.py:76
  26.9 15.6 %copy-start.1 = (bf16[1,1024,384]{2,1,0:T(8,128)(2,1)S(1)}, bf16[1,1024,384]{2,1,0:T(8,128)(2,1)}, u32[]{:S(2)}) copy-start(bf16[1,1024,384]{2,1,0:T(8,128)(2,1)} %param.16) | copy-start | bytes 2359300
  38.5 15.9 %all-to-all-start.1 = ((bf16[8,20,1024]{2,1,0:T(8,128)(2,1)}), bf16[8,20,1024]{2,1,0:T(8,128)(2,1)S(1)}, u32[]{:S(2)}, u32[]{:S(2)}) async-start(bf16[8,20,1024]{2,1,0:T(8,128)(2,1)} %reshape.98), calls=%async_computation.1 | async-start | bytes 786432 | tf_op jit(solution)/shard_map/all_to_all | solution.py:77
  42.0 103.7 %reduce-scatter.3.cloned.1.call-start = ((), (), s32[]{:S(2)}) async-start(), calls=%async_computation.6 | async-start | bytes 1966080 | tf_op jit(solution)/shard_map/reduce_scatter | solution.py:97
  42.5 17.1 %copy-start.2 = (f32[160,384]{1,0:T(8,128)}, f32[160,384]{1,0:T(8,128)S(1)}, u32[]{:S(2)}) copy-start(f32[160,384]{1,0:T(8,128)S(1)} %fusion.3) | copy-start | bytes 737284
  42.8 16.7 %copy-start.3 = (f32[160,384]{1,0:T(8,128)}, f32[160,384]{1,0:T(8,128)S(1)}, u32[]{:S(2)}) copy-start(f32[160,384]{1,0:T(8,128)S(1)} %fusion.6) | copy-start | bytes 737284
  57.8 89.6 %reduce-scatter.5.cloned.1.call-start = ((), (), s32[]{:S(2)}) async-start(), calls=%async_computation.7 | async-start | bytes 1966080 | tf_op jit(solution)/shard_map/reduce_scatter | solution.py:98
  61.3 83.5 %all-to-all-start.3 = ((bf16[8,20,1024]{2,1,0:T(8,128)(2,1)}), bf16[8,20,1024]{2,1,0:T(8,128)(2,1)S(1)}, u32[]{:S(2)}, u32[]{:S(2)}) async-start(bf16[8,20,1024]{2,1,0:T(8,128)(2,1)} %reshape.101), calls=%async_computation.3 | async-start | bytes 786432 | tf_op jit(solution)/shard_map/all_to_all | solution.py:90
Sparse Core Ops, SparseCore 0:
  57.9 36.4 reduce-scatter.2
  97.4 43.6 reduce-scatter.4
where the time goes:
time: 157 us; the launch traced here: 156 us
  blocking collectives  78.5 us (50%)
  waiting for transfers between devices  26.3 us (17%)
  starting transfers between devices  16.8 us (11%)
  between operations  14.2 us (9%)
  matrix products  9.84 us (6%)
  local copies, waits for them, and re-layouts  5.47 us (3%)
  other arithmetic  4.81 us (3%)
    psum x1, blocking collectives, shards(): grad_down = lax.psum(grad_terms[2][None], 'dp')  78.5 us
    all_to_all x1, waiting for transfers between devices, shards(): lax.all_to_all(token_send, 'expert', split_axis=0, concat_axis=0, tiled=T...  11.6 us
    all_to_all x1, waiting for transfers between devices, shards(): lax.all_to_all(cotan_send, 'expert', split_axis=0, concat_axis=0, tiled=T...  11.6 us
    all_to_all x1, starting transfers between devices, shards(): lax.all_to_all(weight_send, 'expert', split_axis=0, concat_axis=0, tiled=...  6.35 us
    all_to_all x1, starting transfers between devices, shards(): lax.all_to_all(grad_rows, 'expert', split_axis=0, concat_axis=0, tiled=True)  3.46 us
    all_to_all x1, starting transfers between devices, shards(): lax.all_to_all(token_send, 'expert', split_axis=0, concat_axis=0, tiled=T...  3.45 us
    all_to_all x1, starting transfers between devices, shards(): lax.all_to_all(cotan_send, 'expert', split_axis=0, concat_axis=0, tiled=T...  3.45 us
  transfers between devices with their start and end apart: 6, of which 3 were waited for; matrix products, arithmetic and copies ran while one was open for 7% of the time, Pallas kernels for 0%

commit v1 on v0

--- a/solution.py
+++ b/solution.py
@@ -1,6 +1,10 @@
+import functools
+
 import jax
 import jax.numpy as jnp
 from jax import lax
+from jax.experimental import pallas as pl
+from jax.experimental.pallas import tpu as pltpu
 from jax.sharding import PartitionSpec as P
 
 
@@ -106,6 +110,429 @@
     )
 
 
+MESH = pl.DeviceIdType.MESH
+LANES = 128
+TILE = 16
+NT = (((1,), (1,)), ((), ()))
+TN = (((0,), (0,)), ((), ()))
+
+
+def slots_of(token_count, route_count, expert_count):
+    capacity = max(2, min(token_count * route_count * 7 // (8 * expert_count), token_count // 2))
+    return capacity, 2 * max(1, capacity // 6)
+
+
+def dense_fits(sizes, token_count, features, route_count, hidden_size):
+    capacity, spare = slots_of(token_count, route_count, sizes["expert"])
+    return (
+        route_count == sizes["expert"]
+        and sizes["dp"] == 4
+        and sizes["expert"] % 2 == 0
+        and token_count == 2 * TILE
+        and capacity == TILE
+        and spare * 2 == 8
+        and features % (8 * LANES) == 0
+        and hidden_size % LANES == 0
+    )
+
+
+def dense_kernel(
+    experts,
+    tok_ref,
+    cot_ref,
+    routes_ref,
+    comb_ref,
+    hot_ref,
+    extra_ref,
+    wg_hbm,
+    wu_hbm,
+    wd_hbm,
+    tg_ref,
+    gg_out,
+    gu_out,
+    gd_out,
+    slab,
+    wg,
+    wu,
+    wd,
+    all_t,
+    all_og,
+    all_h,
+    all_gg,
+    all_ug,
+    row_out,
+    pair_in,
+    pair_sum,
+    z_in,
+    w_sem,
+    send_sem,
+    recv_sem,
+    pair_send,
+    pair_recv,
+    z_send,
+    z_recv,
+):
+    levels = experts // 2
+    features = tok_ref.shape[1]
+    blocks = features // LANES
+    half = blocks // 2
+    spill_at = 2 * blocks
+    weight_at = spill_at + half
+    bf16, f32 = jnp.bfloat16, jnp.float32
+
+    d = lax.axis_index("dp")
+    e = lax.axis_index("expert")
+    z, c = e // 2, e % 2
+    dx = d + 1 - 2 * (d % 2)
+    dy = (d + 2) % 4
+    dd = 3 - d
+    pc = 1 - c
+
+    def to(dp, level, core):
+        return (dp, level * 2 + core)
+
+    def slab_id(dp, level, core):
+        return dp * experts + level * 2 + core
+
+    weight_copies = [
+        pltpu.make_async_copy(h.at[0], v, w_sem.at[i])
+        for i, (h, v) in enumerate(((wg_hbm, wg), (wu_hbm, wu), (wd_hbm, wd)))
+    ]
+    for copy in weight_copies:
+        copy.start()
+
+    barrier = pltpu.get_barrier_semaphore()
+    for peer in (to(dx, z, c), to(dy, z, c), to(d, z, pc)):
+        pl.semaphore_signal(barrier, inc=1, device_id=peer, device_id_type=MESH)
+    for step in range(1, levels):
+        pl.semaphore_signal(
+            barrier, inc=1, device_id=to(d, (z + step) % levels, c), device_id_type=MESH
+        )
+
+    me = slab_id(d, z, c)
+    lane = lax.broadcasted_iota(jnp.int32, (2 * TILE, LANES), 1)
+    row = lax.broadcasted_iota(jnp.int32, (2 * TILE, LANES), 0)
+    routes = routes_ref[...]
+    comb = comb_ref[...].astype(f32)
+    weights = jnp.zeros((2 * TILE, LANES), f32)
+    for k in range(routes.shape[1]):
+        weights = jnp.where(lane == routes[:, k : k + 1], comb[:, k : k + 1], weights)
+    limit = jnp.full((2 * TILE, LANES), TILE, jnp.int32)
+    for j in range(hot_ref.shape[0]):
+        limit = limit + jnp.where(lane == hot_ref[j], extra_ref[j], 0)
+    weights = jnp.where(row < limit, weights, 0.0).astype(bf16)
+    slab[me, weight_at] = weights[:TILE]
+    slab[me, weight_at + 1] = weights[TILE:]
+    tok_tail = tok_ref[TILE:, :].astype(f32)[:8]
+    cot_tail = cot_ref[TILE:, :].astype(f32)[:8]
+    tail_row = lax.broadcasted_iota(jnp.int32, (8, features), 0)
+    spill = jnp.where(tail_row < 4, tok_tail, pltpu.roll(cot_tail, 4, 0))
+    for j in range(blocks):
+        cols = slice(j * LANES, (j + 1) * LANES)
+        slab[me, j] = tok_ref[:TILE, cols]
+        slab[me, blocks + j] = cot_ref[:TILE, cols]
+    for j in range(half):
+        lo = spill[:, j * LANES : (j + 1) * LANES]
+        hi = spill[:, (half + j) * LANES : (half + j + 1) * LANES]
+        slab[me, spill_at + j] = jnp.concatenate([lo, hi], axis=0).astype(bf16)
+
+    pl.semaphore_wait(barrier, 3 + levels - 1)
+
+    def copy_of(s, way, peer):
+        return pltpu.make_async_remote_copy(
+            src_ref=slab.at[s],
+            dst_ref=slab.at[s],
+            send_sem=send_sem.at[way, s],
+            recv_sem=recv_sem.at[s],
+            device_id=peer,
+            device_id_type=MESH,
+        )
+
+    def to_x(s):
+        return copy_of(s, 0, to(dx, z, c))
+
+    def to_y(s):
+        return copy_of(s, 1, to(dy, z, c))
+
+    def to_pair(s):
+        return copy_of(s, 2, to(d, z, pc))
+
+    def to_up(s):
+        return copy_of(s, 3, to(d, z + 1, c))
+
+    def to_down(s):
+        return copy_of(s, 4, to(d, z - 1, c))
+
+    def arrived(s):
+        to_pair(s).wait_recv()
+
+    @pl.when(z + 1 < levels)
+    def _():
+        to_up(me).start()
+
+    @pl.when(z > 0)
+    def _():
+        to_down(me).start()
+
+    to_x(me).start()
+    to_y(me).start()
+    to_pair(me).start()
+
+    for dist in range(1, levels):
+
+        @pl.when(z - dist >= 0)
+        def _():
+            s = slab_id(d, z - dist, c)
+            arrived(s)
+
+            @pl.when(z + 1 < levels)
+            def _():
+                to_up(s).start()
+
+            to_x(s).start()
+            to_y(s).start()
+            to_pair(s).start()
+
+        @pl.when(z + dist < levels)
+        def _():
+            s = slab_id(d, z + dist, c)
+            arrived(s)
+
+            @pl.when(z > 0)
+            def _():
+                to_down(s).start()
+
+            to_x(s).start()
+            to_y(s).start()
+            to_pair(s).start()
+
+    for level in range(levels):
+        arrived(slab_id(d, level, pc))
+
+    main_rows = experts * TILE
+    group_rows = main_rows + experts * 8
+    own_lane = lax.broadcasted_iota(jnp.int32, (group_rows, LANES), 1) == e
+
+    def group(dp, at):
+        rows = pl.ds(at, group_rows)
+        part = pl.ds(dp * experts, experts)
+
+        def main(j):
+            return slab[part, j].reshape(main_rows, LANES)
+
+        lo, hi = [], []
+        for j in range(half):
+            both = slab[part, spill_at + j].astype(f32)
+            lo.append(both[:, :8].reshape(experts * 8, LANES))
+            hi.append(both[:, 8:].reshape(experts * 8, LANES))
+        tail = jnp.concatenate(lo + hi, axis=1)
+        cot_rows = pltpu.roll(tail, experts * 8 - 4, 0)
+        w_main = main(weight_at).astype(f32)
+        w_tail = slab[part, weight_at + 1].astype(f32)[:, :8].reshape(experts * 8, LANES)
+        w = jnp.sum(
+            jnp.where(own_lane, jnp.concatenate([w_main, w_tail], axis=0), 0.0),
+            axis=1,
+            keepdims=True,
+        )
+        all_t[rows, :] = jnp.concatenate(
+            [jnp.concatenate([main(j) for j in range(blocks)], axis=1), tail.astype(bf16)], axis=0
+        )
+        cot = jnp.concatenate(
+            [
+                jnp.concatenate([main(blocks + j) for j in range(blocks)], axis=1).astype(f32),
+                cot_rows,
+            ],
+            axis=0,
+        )
+        all_og[rows, :] = (w * cot).astype(bf16)
+        t = all_t[rows, :]
+        gate_pre = jnp.dot(t, wg[...], preferred_element_type=f32)
+        up_proj = jnp.dot(t, wu[...], preferred_element_type=f32)
+        hidden_grad = lax.dot_general(all_og[rows, :], wd[...], NT, preferred_element_type=f32)
+        sig = jax.nn.sigmoid(gate_pre)
+        act = gate_pre * sig
+        all_h[rows, :] = (act * up_proj).astype(bf16)
+        all_gg[rows, :] = (hidden_grad * up_proj * sig * (1.0 + gate_pre * (1.0 - sig))).astype(
+            bf16
+        )
+        all_ug[rows, :] = (hidden_grad * act).astype(bf16)
+
+    for copy in weight_copies:
+        copy.wait()
+    group(d, 0)
+    own = pl.ds(0, group_rows)
+    rg = lax.dot_general(all_gg[own, :], wg[...], NT, preferred_element_type=f32)
+    rg = rg + lax.dot_general(all_ug[own, :], wu[...], NT, preferred_element_type=f32)
+    for j in range(blocks):
+        row_out[:, j] = (
+            rg[:main_rows, j * LANES : (j + 1) * LANES].reshape(experts, TILE, LANES).astype(bf16)
+        )
+    for j in range(half):
+        lo = rg[main_rows:, j * LANES : (j + 1) * LANES].reshape(experts, 8, LANES)
+        hi = rg[main_rows:, (half + j) * LANES : (half + j + 1) * LANES].reshape(experts, 8, LANES)
+        row_out[:, blocks + j] = jnp.concatenate([lo, hi], axis=1).astype(bf16)
+
+    def pair_copy(level):
+        return pltpu.make_async_remote_copy(
+            src_ref=row_out.at[level * 2 + pc],
+            dst_ref=pair_in.at[level],
+            send_sem=pair_send.at[level],
+            recv_sem=pair_recv.at[level],
+            device_id=to(d, z, pc),
+            device_id_type=MESH,
+        )
+
+    for level in range(levels):
+        pair_copy(level).start()
+
+    for level in range(levels):
+        s = slab_id(dx, level, c)
+        arrived(s)
+        if level % 2 == 0:
+            to_y(s).start()
+        to_pair(s).start()
+        s = slab_id(dy, level, c)
+        arrived(s)
+        if level % 2 == 1:
+            to_x(s).start()
+        to_pair(s).start()
+
+    for level in range(levels):
+        pair_copy(level).wait_recv()
+        pair_sum[level] = (
+            row_out[level * 2 + c].astype(f32) + pair_in[level].astype(f32)
+        ).astype(bf16)
+
+    def z_copy(step):
+        level = (z + step) % levels
+        return pltpu.make_async_remote_copy(
+            src_ref=pair_sum.at[level],
+            dst_ref=z_in.at[step - 1],
+            send_sem=z_send.at[step - 1],
+            recv_sem=z_recv.at[step - 1],
+            device_id=to(d, level, c),
+            device_id_type=MESH,
+        )
+
+    for step in range(1, levels):
+        z_copy(step).start()
+
+    for level in range(levels):
+        arrived(slab_id(dx, level, pc))
+    group(dx, group_rows)
+    for level in range(levels):
+        s = slab_id(dd, level, c)
+        arrived(s)
+        to_pair(s).start()
+    for level in range(levels):
+        arrived(slab_id(dy, level, pc))
+    group(dy, 2 * group_rows)
+    for level in range(levels):
+        arrived(slab_id(dd, level, pc))
+    group(dd, 3 * group_rows)
+
+    share = features // 4
+    t_cols = all_t[:, pl.ds(pl.multiple_of(d * share, LANES), share)]
+    gg_out[0] = lax.dot_general(t_cols, all_gg[...], TN, preferred_element_type=f32).astype(bf16)
+    gu_out[0] = lax.dot_general(t_cols, all_ug[...], TN, preferred_element_type=f32).astype(bf16)
+    gd_out[0] = lax.dot_general(all_h[...], all_og[...], TN, preferred_element_type=f32).astype(
+        bf16
+    )
+
+    total = pair_sum[z].astype(f32)
+    for step in range(1, levels):
+        z_copy(step).wait_recv()
+        total = total + z_in[step - 1].astype(f32)
+    for j in range(blocks):
+        tg_ref[:TILE, j * LANES : (j + 1) * LANES] = total[j].astype(bf16)
+    blank = jnp.zeros((8, LANES), f32)
+    for j in range(half):
+        tile = total[blocks + j]
+        tg_ref[TILE:, j * LANES : (j + 1) * LANES] = jnp.concatenate(
+            [tile[:8], blank], axis=0
+        ).astype(bf16)
+        tg_ref[TILE:, (half + j) * LANES : (half + j + 1) * LANES] = jnp.concatenate(
+            [tile[8:], blank], axis=0
+        ).astype(bf16)
+
+    for level in range(levels):
+        s = slab_id(d, level, c)
+        to_x(s).wait_send()
+        to_y(s).wait_send()
+        to_pair(s).wait_send()
+        if level % 2 == 0:
+            to_y(slab_id(dx, level, c)).wait_send()
+        else:
+            to_x(slab_id(dy, level, c)).wait_send()
+        for dp in (dx, dy, dd):
+            to_pair(slab_id(dp, level, c)).wait_send()
+        pair_copy(level).wait_send()
+
+        @pl.when((z >= level) & (z + 1 < levels))
+        def _():
+            to_up(s).wait_send()
+
+        @pl.when((z <= level) & (z > 0))
+        def _():
+            to_down(s).wait_send()
+
+    for step in range(1, levels):
+        z_copy(step).wait_send()
+
+
+def dense_shards(tokens, cotangent, routes, combine, hot_experts, extra_slots, w_gate, w_up, w_down):
+    experts = lax.axis_size("expert")
+    replicas = lax.axis_size("dp")
+    token_count, features = tokens.shape
+    hidden_size = w_gate.shape[2]
+    blocks = features // LANES
+    levels = experts // 2
+    tiles = 2 * blocks + blocks // 2 + 2
+    back = blocks + blocks // 2
+    rows = replicas * experts * (TILE + 8)
+    bf16 = jnp.bfloat16
+    vmem = pl.BlockSpec(memory_space=pltpu.VMEM)
+    smem = pl.BlockSpec(memory_space=pltpu.SMEM)
+    hbm = pl.BlockSpec(memory_space=pl.ANY)
+    dma = pltpu.SemaphoreType.DMA
+    return pl.pallas_call(
+        functools.partial(dense_kernel, experts),
+        out_shape=(
+            jax.ShapeDtypeStruct((token_count, features), bf16),
+            jax.ShapeDtypeStruct((1, features // replicas, hidden_size), bf16),
+            jax.ShapeDtypeStruct((1, features // replicas, hidden_size), bf16),
+            jax.ShapeDtypeStruct((1, hidden_size, features), bf16),
+        ),
+        in_specs=[vmem, vmem, vmem, vmem, smem, smem, hbm, hbm, hbm],
+        out_specs=(vmem, vmem, vmem, vmem),
+        scratch_shapes=[
+            pltpu.VMEM((replicas * experts, tiles, TILE, LANES), bf16),
+            pltpu.VMEM((features, hidden_size), bf16),
+            pltpu.VMEM((features, hidden_size), bf16),
+            pltpu.VMEM((hidden_size, features), bf16),
+            pltpu.VMEM((rows, features), bf16),
+            pltpu.VMEM((rows, features), bf16),
+            pltpu.VMEM((rows, hidden_size), bf16),
+            pltpu.VMEM((rows, hidden_size), bf16),
+            pltpu.VMEM((rows, hidden_size), bf16),
+            pltpu.VMEM((experts, back, TILE, LANES), bf16),
+            pltpu.VMEM((levels, back, TILE, LANES), bf16),
+            pltpu.VMEM((levels, back, TILE, LANES), bf16),
+            pltpu.VMEM((levels - 1, back, TILE, LANES), bf16),
+            dma((3,)),
+            dma((5, replicas * experts)),
+            dma((replicas * experts,)),
+            dma((levels,)),
+            dma((levels,)),
+            dma((levels - 1,)),
+            dma((levels - 1,)),
+        ],
+        compiler_params=pltpu.CompilerParams(
+            collective_id=0, has_side_effects=True, vmem_limit_bytes=48 * 1024 * 1024
+        ),
+    )(tokens, cotangent, routes, combine, hot_experts, extra_slots, w_gate, w_up, w_down)
+
+
 def solution(mesh):
     in_specs = (
         P(("dp", "expert"), None),
@@ -124,4 +551,11 @@
         P("expert", "dp", None),
         P("expert", None, None),
     )
-    return jax.shard_map(shards, mesh=mesh, in_specs=in_specs, out_specs=out_specs, check_vma=False)
+
+    def body(*args):
+        token_count, features = args[0].shape
+        if dense_fits(dict(mesh.shape), token_count, features, args[2].shape[1], args[6].shape[2]):
+            return dense_shards(*args)
+        return shards(*args)
+
+    return jax.shard_map(body, mesh=mesh, in_specs=in_specs, out_specs=out_specs, check_vma=False)

time: 157 us -> 39.7 us (0.25)
  blocking collectives: 78.5 us -> 0 us
  Pallas kernels: 0 us -> 29.3 us
  waiting for transfers between devices: 26.3 us -> 0 us
  starting transfers between devices: 16.8 us -> 0 us
  between operations: 14.2 us -> 0.66 us
  matrix products: 9.84 us -> 0 us
  other arithmetic: 4.81 us -> 0 us
  local copies, waits for them, and re-layouts: 5.47 us -> 9.38 us
    psum x1 -> x0, blocking collectives: 78.5 us -> none  [shards(): grad_down = lax.psum(grad_terms[2][None], 'dp')]
    pallas_call x0 -> x1, Pallas kernels: none -> 29.3 us  [dense_shards(): pl.pallas_call(functools.partial(dense_kernel, experts), out_shape=(jax.S...]
    all_to_all x4 -> x0, waiting for transfers between devices: 26.3 us -> none  [the longest x1 11.6 us: shards(): lax.all_to_all(token_send, 'expert', split_axis=0, concat_axis=0, tiled=T...]
    all_to_all x4 -> x0, starting transfers between devices: 16.7 us -> none  [the longest x1 6.35 us: shards(): lax.all_to_all(weight_send, 'expert', split_axis=0, concat_axis=0, tiled=...]
    dot_general x10 -> x0, matrix products: 9.84 us -> none  [the longest x1 1.63 us: weight_terms(): jnp.dot(row_tokens.T, gate_grad, preferred_element_type=jnp.float32)]
    unnamed x9 -> x22, local copies, waits for them, and re-layouts: 0.86 us -> 9.38 us
    convert_element_type x5 -> x0, other arithmetic: 3.54 us -> none  [the longest x1 1.7 us: shards(): grad_gate.astype(jnp.bfloat16)]
    reshape x5 -> x0, local copies, waits for them, and re-layouts: 2.57 us -> none  [the longest x1 0.81 us: shards(): filled[:, :features].reshape(expert_count, slot_count, features)]
  transfers between devices with their start and end apart: 6 -> 0, of which waited for: 3 -> 0; matrix products, arithmetic and copies ran while one was open for 7% -> 0% of each run, Pallas kernels for 0% -> 0%
where the time goes in v1:
time: 39.7 us; the launch traced here: 39.3 us
  Pallas kernels  29.3 us (74%)
  local copies, waits for them, and re-layouts  9.38 us (24%)
  between operations  0.66 us (2%)
    pallas_call x1, Pallas kernels, dense_shards(): pl.pallas_call(functools.partial(dense_kernel, experts), out_shape=(jax.S...  29.3 us
    unnamed x22, local copies, waits for them, and re-layouts  9.38 us

profile of v1, /device:TPU:0, one launch (start us, length us, event | category | flops | bytes accessed | tf_op | source)
XLA Modules:
  0.0 39.3 jit_solution(10242696160410986099)
XLA Ops:
  0.6 0.0 copy-start.7
  0.6 0.8 %copy.14.comb_ref = bf16[32,8]{1,0:T(8,128)(2,1)S(1)} copy(bf16[32,8]{0,1:T(8,128)(2,1)} %param.12) | data formatting | bytes 1024 | tf_op args[3]
  1.4 0.0 copy-done.7
  1.4 0.0 copy-start.5
  1.4 0.0 copy-start.6
  1.4 0.1 copy.13.routes_ref
  1.5 0.6 %copy-done.5 = s32[4]{0:T(128)S(1)} copy-done((s32[4]{0:T(128)S(1)}, s32[4]{0:T(128)}, u32[]{:S(2)}) %copy-start.5) | copy-done | bytes 40
  2.1 0.0 copy-done.6
  2.1 0.0 copy-start
  2.1 1.1 %copy-done = bf16[1,1024,384]{2,1,0:T(8,128)(2,1)S(1)} copy-done((bf16[1,1024,384]{2,1,0:T(8,128)(2,1)S(1)}, bf16[1,1024,384]{2,1,0:T(8,128)(2,1)}, u32[]{:S(2)}) %copy-start) | copy-done | bytes 786456
  3.2 0.0 copy-start.1
  3.2 1.1 %copy-done.1 = bf16[1,1024,384]{2,1,0:T(8,128)(2,1)S(1)} copy-done((bf16[1,1024,384]{2,1,0:T(8,128)(2,1)S(1)}, bf16[1,1024,384]{2,1,0:T(8,128)(2,1)}, u32[]{:S(2)}) %copy-start.1) | copy-done | bytes 786456
  4.4 0.0 copy-start.2
  4.4 1.1 %copy-done.2 = bf16[1,384,1024]{2,1,0:T(8,128)(2,1)S(1)} copy-done((bf16[1,384,1024]{2,1,0:T(8,128)(2,1)S(1)}, bf16[1,384,1024]{2,1,0:T(8,128)(2,1)}, u32[]{:S(2)}) %copy-start.2) | copy-done | bytes 786456
  5.5 0.0 copy-start.3
  5.5 0.8 %copy-done.3 = bf16[32,1024]{1,0:T(8,128)(2,1)S(1)} copy-done((bf16[32,1024]{1,0:T(8,128)(2,1)S(1)}, bf16[32,1024]{1,0:T(8,128)(2,1)}, u32[]{:S(2)}) %copy-start.3) | copy-done | bytes 65560
  6.3 0.0 copy-start.4
  6.3 0.8 %copy-done.4 = bf16[32,1024]{1,0:T(8,128)(2,1)S(1)} copy-done((bf16[32,1024]{1,0:T(8,128)(2,1)S(1)}, bf16[32,1024]{1,0:T(8,128)(2,1)}, u32[]{:S(2)}) %copy-start.4) | copy-done | bytes 65560
  7.2 29.3 %shard_map.120 = (bf16[32,1024]{1,0:T(8,128)(2,1)S(1)}, bf16[1,256,384]{2,1,0:T(8,128)(2,1)S(1)}, bf16[1,256,384]{2,1,0:T(8,128)(2,1)S(1)}, bf16[1,384,1024]{2,1,0:T(8,128)(2,1)S(1)}) custom-call(bf16[32,1024]{1,0:T(8,128)(2,1)S(1)} %copy-done.3, bf16[32,1024]{1,0:T(8,128)(2,1)S(1)} %copy-done.4, s32[32,8]{1,0:T(8,128)S(1)} %copy.13.routes_ref, ...), custom_call_target="tpu_custom_call" | custom-call | tf_op jit(solution)/shard_map/pallas_call | solution.py:498
  36.4 0.6 %copy.19 = bf16[32,1024]{1,0:T(8,128)(2,1)} copy(bf16[32,1024]{1,0:T(8,128)(2,1)S(1)} %get-tuple-element.8) | data formatting | bytes 131072
  37.1 0.7 %copy.20 = bf16[1,256,384]{2,1,0:T(8,128)(2,1)} copy(bf16[1,256,384]{2,1,0:T(8,128)(2,1)S(1)} %get-tuple-element.9) | data formatting | bytes 393216
  37.8 0.7 %copy.21 = bf16[1,256,384]{2,1,0:T(8,128)(2,1)} copy(bf16[1,256,384]{2,1,0:T(8,128)(2,1)S(1)} %get-tuple-element.10) | data formatting | bytes 393216
  38.4 0.9 %copy.22 = bf16[1,384,1024]{2,1,0:T(8,128)(2,1)} copy(bf16[1,384,1024]{2,1,0:T(8,128)(2,1)S(1)} %get-tuple-element.11) | data formatting | bytes 1572864
Async XLA Ops:
  0.6 0.8 %copy-start.7 = (s32[32,8]{0,1:T(8,128)S(1)}, s32[32,8]{0,1:T(8,128)}, u32[]{:S(2)}) copy-start(s32[32,8]{0,1:T(8,128)} %param.11) | copy-start | bytes 3076
  1.4 0.7 %copy-start.5 = (s32[4]{0:T(128)S(1)}, s32[4]{0:T(128)}, u32[]{:S(2)}) copy-start(s32[4]{0:T(128)} %hot_ref.1) | copy-start | bytes 52
  1.4 0.7 %copy-start.6 = (s32[4]{0:T(128)S(1)}, s32[4]{0:T(128)}, u32[]{:S(2)}) copy-start(s32[4]{0:T(128)} %extra_ref.1) | copy-start | bytes 52
  2.1 1.1 %copy-start = (bf16[1,1024,384]{2,1,0:T(8,128)(2,1)S(1)}, bf16[1,1024,384]{2,1,0:T(8,128)(2,1)}, u32[]{:S(2)}) copy-start(bf16[1,1024,384]{2,1,0:T(8,128)(2,1)} %wg_hbm.1) | copy-start | bytes 2359300
  3.2 1.1 %copy-start.1 = (bf16[1,1024,384]{2,1,0:T(8,128)(2,1)S(1)}, bf16[1,1024,384]{2,1,0:T(8,128)(2,1)}, u32[]{:S(2)}) copy-start(bf16[1,1024,384]{2,1,0:T(8,128)(2,1)} %wu_hbm.1) | copy-start | bytes 2359300
  4.4 1.1 %copy-start.2 = (bf16[1,384,1024]{2,1,0:T(8,128)(2,1)S(1)}, bf16[1,384,1024]{2,1,0:T(8,128)(2,1)}, u32[]{:S(2)}) copy-start(bf16[1,384,1024]{2,1,0:T(8,128)(2,1)} %wd_hbm.1) | copy-start | bytes 2359300
  5.5 0.8 %copy-start.3 = (bf16[32,1024]{1,0:T(8,128)(2,1)S(1)}, bf16[32,1024]{1,0:T(8,128)(2,1)}, u32[]{:S(2)}) copy-start(bf16[32,1024]{1,0:T(8,128)(2,1)} %tok_ref.1) | copy-start | bytes 196612
  6.3 0.8 %copy-start.4 = (bf16[32,1024]{1,0:T(8,128)(2,1)S(1)}, bf16[32,1024]{1,0:T(8,128)(2,1)}, u32[]{:S(2)}) copy-start(bf16[32,1024]{1,0:T(8,128)(2,1)} %cot_ref.1) | copy-start | bytes 196612

commit v2 on v1

--- a/solution.py
+++ b/solution.py
@@ -138,12 +138,12 @@
 
 def dense_kernel(
     experts,
-    tok_ref,
-    cot_ref,
-    routes_ref,
-    comb_ref,
-    hot_ref,
-    extra_ref,
+    tok_hbm,
+    cot_hbm,
+    routes_hbm,
+    comb_hbm,
+    hot_hbm,
+    extra_hbm,
     wg_hbm,
     wu_hbm,
     wd_hbm,
@@ -151,6 +151,13 @@
     gg_out,
     gu_out,
     gd_out,
+    tok_ref,
+    cot_ref,
+    routes_ref,
+    comb_ref,
+    hot_ref,
+    extra_ref,
+    in_sem,
     slab,
     wg,
     wu,
@@ -160,6 +167,9 @@
     all_h,
     all_gg,
     all_ug,
+    acc_gate,
+    acc_up,
+    acc_down,
     row_out,
     pair_in,
     pair_sum,
@@ -194,6 +204,21 @@
     def slab_id(dp, level, core):
         return dp * experts + level * 2 + core
 
+    input_copies = [
+        pltpu.make_async_copy(h, v, in_sem.at[i])
+        for i, (h, v) in enumerate(
+            (
+                (tok_hbm, tok_ref),
+                (cot_hbm, cot_ref),
+                (routes_hbm, routes_ref),
+                (comb_hbm, comb_ref),
+                (hot_hbm, hot_ref),
+                (extra_hbm, extra_ref),
+            )
+        )
+    ]
+    for copy in input_copies:
+        copy.start()
     weight_copies = [
         pltpu.make_async_copy(h.at[0], v, w_sem.at[i])
         for i, (h, v) in enumerate(((wg_hbm, wg), (wu_hbm, wu), (wd_hbm, wd)))
@@ -210,17 +235,26 @@
         )
 
     me = slab_id(d, z, c)
-    lane = lax.broadcasted_iota(jnp.int32, (2 * TILE, LANES), 1)
-    row = lax.broadcasted_iota(jnp.int32, (2 * TILE, LANES), 0)
+    for copy in input_copies:
+        copy.wait()
+    names = -(-experts // TILE) * TILE
+    expert_row = lax.broadcasted_iota(jnp.int32, (names, 2 * TILE), 0)
+    token_lane = lax.broadcasted_iota(jnp.int32, (names, 2 * TILE), 1)
     routes = routes_ref[...]
     comb = comb_ref[...].astype(f32)
-    weights = jnp.zeros((2 * TILE, LANES), f32)
-    for k in range(routes.shape[1]):
-        weights = jnp.where(lane == routes[:, k : k + 1], comb[:, k : k + 1], weights)
-    limit = jnp.full((2 * TILE, LANES), TILE, jnp.int32)
+    weights = jnp.zeros((names, 2 * TILE), f32)
+    for r in range(routes.shape[0]):
+        weights = jnp.where(expert_row == routes[r : r + 1, :], comb[r : r + 1, :], weights)
+    limit = jnp.full((names, 2 * TILE), TILE, jnp.int32)
     for j in range(hot_ref.shape[0]):
-        limit = limit + jnp.where(lane == hot_ref[j], extra_ref[j], 0)
-    weights = jnp.where(row < limit, weights, 0.0).astype(bf16)
+        limit = limit + jnp.where(expert_row == hot_ref[j], extra_ref[j], 0)
+    weights = jnp.where(token_lane < limit, weights, 0.0).astype(bf16)
+    unit = lax.broadcasted_iota(jnp.int32, (names, LANES), 0) == lax.broadcasted_iota(
+        jnp.int32, (names, LANES), 1
+    )
+    weights = lax.dot_general(
+        weights, jnp.where(unit, 1.0, 0.0).astype(bf16), TN, preferred_element_type=f32
+    ).astype(bf16)
     slab[me, weight_at] = weights[:TILE]
     slab[me, weight_at + 1] = weights[TILE:]
     tok_tail = tok_ref[TILE:, :].astype(f32)[:8]
@@ -427,17 +461,26 @@
     for level in range(levels):
         arrived(slab_id(dy, level, pc))
     group(dy, 2 * group_rows)
+    share = features // 4
+
+    def weight_terms(at, count):
+        rows = pl.ds(at, count)
+        t_cols = all_t[rows, pl.ds(pl.multiple_of(d * share, LANES), share)]
+        return (
+            lax.dot_general(t_cols, all_gg[rows, :], TN, preferred_element_type=f32),
+            lax.dot_general(t_cols, all_ug[rows, :], TN, preferred_element_type=f32),
+            lax.dot_general(all_h[rows, :], all_og[rows, :], TN, preferred_element_type=f32),
+        )
+
+    early = weight_terms(0, 3 * group_rows)
+    acc_gate[...], acc_up[...], acc_down[...] = early
     for level in range(levels):
         arrived(slab_id(dd, level, pc))
     group(dd, 3 * group_rows)
-
-    share = features // 4
-    t_cols = all_t[:, pl.ds(pl.multiple_of(d * share, LANES), share)]
-    gg_out[0] = lax.dot_general(t_cols, all_gg[...], TN, preferred_element_type=f32).astype(bf16)
-    gu_out[0] = lax.dot_general(t_cols, all_ug[...], TN, preferred_element_type=f32).astype(bf16)
-    gd_out[0] = lax.dot_general(all_h[...], all_og[...], TN, preferred_element_type=f32).astype(
-        bf16
-    )
+    late = weight_terms(3 * group_rows, group_rows)
+    gg_out[0] = (acc_gate[...] + late[0]).astype(bf16)
+    gu_out[0] = (acc_up[...] + late[1]).astype(bf16)
+    gd_out[0] = (acc_down[...] + late[2]).astype(bf16)
 
     total = pair_sum[z].astype(f32)
     for step in range(1, levels):
@@ -480,6 +523,18 @@
         z_copy(step).wait_send()
 
 
+def write_kernel(*refs):
+    sources, sem = refs[: len(refs) // 2], refs[-1]
+    targets = refs[len(refs) // 2 : -1]
+    copies = [
+        pltpu.make_async_copy(a, b, sem.at[i]) for i, (a, b) in enumerate(zip(sources, targets))
+    ]
+    for copy in copies:
+        copy.start()
+    for copy in copies:
+        copy.wait()
+
+
 def dense_shards(tokens, cotangent, routes, combine, hot_experts, extra_slots, w_gate, w_up, w_down):
     experts = lax.axis_size("expert")
     replicas = lax.axis_size("dp")
@@ -492,10 +547,23 @@
     rows = replicas * experts * (TILE + 8)
     bf16 = jnp.bfloat16
     vmem = pl.BlockSpec(memory_space=pltpu.VMEM)
-    smem = pl.BlockSpec(memory_space=pltpu.SMEM)
-    hbm = pl.BlockSpec(memory_space=pl.ANY)
+    hbm = pl.BlockSpec(memory_space=pltpu.HBM)
     dma = pltpu.SemaphoreType.DMA
-    return pl.pallas_call(
+    operands = [
+        pltpu.with_memory_space_constraint(a, pltpu.HBM)
+        for a in (
+            tokens,
+            cotangent,
+            routes.T,
+            combine.T,
+            hot_experts,
+            extra_slots,
+            w_gate,
+            w_up,
+            w_down,
+        )
+    ]
+    results = pl.pallas_call(
         functools.partial(dense_kernel, experts),
         out_shape=(
             jax.ShapeDtypeStruct((token_count, features), bf16),
@@ -503,9 +571,16 @@
             jax.ShapeDtypeStruct((1, features // replicas, hidden_size), bf16),
             jax.ShapeDtypeStruct((1, hidden_size, features), bf16),
         ),
-        in_specs=[vmem, vmem, vmem, vmem, smem, smem, hbm, hbm, hbm],
+        in_specs=[hbm] * 9,
         out_specs=(vmem, vmem, vmem, vmem),
         scratch_shapes=[
+            pltpu.VMEM(tokens.shape, bf16),
+            pltpu.VMEM(tokens.shape, bf16),
+            pltpu.VMEM(routes.shape[::-1], jnp.int32),
+            pltpu.VMEM(routes.shape[::-1], bf16),
+            pltpu.SMEM(hot_experts.shape, jnp.int32),
+            pltpu.SMEM(hot_experts.shape, jnp.int32),
+            dma((6,)),
             pltpu.VMEM((replicas * experts, tiles, TILE, LANES), bf16),
             pltpu.VMEM((features, hidden_size), bf16),
             pltpu.VMEM((features, hidden_size), bf16),
@@ -515,6 +590,9 @@
             pltpu.VMEM((rows, hidden_size), bf16),
             pltpu.VMEM((rows, hidden_size), bf16),
             pltpu.VMEM((rows, hidden_size), bf16),
+            pltpu.VMEM((features // replicas, hidden_size), jnp.float32),
+            pltpu.VMEM((features // replicas, hidden_size), jnp.float32),
+            pltpu.VMEM((hidden_size, features), jnp.float32),
             pltpu.VMEM((experts, back, TILE, LANES), bf16),
             pltpu.VMEM((levels, back, TILE, LANES), bf16),
             pltpu.VMEM((levels, back, TILE, LANES), bf16),
@@ -528,9 +606,17 @@
             dma((levels - 1,)),
         ],
         compiler_params=pltpu.CompilerParams(
-            collective_id=0, has_side_effects=True, vmem_limit_bytes=48 * 1024 * 1024
+            collective_id=0, has_side_effects=True, vmem_limit_bytes=32 * 1024 * 1024
         ),
-    )(tokens, cotangent, routes, combine, hot_experts, extra_slots, w_gate, w_up, w_down)
+    )(*operands)
+    return pl.pallas_call(
+        write_kernel,
+        out_shape=tuple(jax.ShapeDtypeStruct(r.shape, r.dtype) for r in results),
+        in_specs=[vmem] * len(results),
+        out_specs=tuple(hbm for _ in results),
+        scratch_shapes=[dma((len(results),))],
+        compiler_params=pltpu.CompilerParams(vmem_limit_bytes=8 * 1024 * 1024),
+    )(*results)
 
 
 def solution(mesh):

time: 39.7 us -> 31 us (0.78)
  local copies, waits for them, and re-layouts: 9.38 us -> 0 us
  Pallas kernels: 29.3 us -> 30.2 us
    unnamed x22 -> x0, local copies, waits for them, and re-layouts: 9.38 us -> none
    pallas_call x0 -> x1, Pallas kernels: none -> 1.07 us  [dense_shards(): pl.pallas_call(write_kernel, out_shape=tuple((jax.ShapeDtypeStruct(r.shap...]
where the time goes in v2:
time: 31 us; the launch traced here: 30.8 us
  Pallas kernels  30.2 us (97%)
  between operations  0.64 us (2%)
    pallas_call x1, Pallas kernels, dense_shards(): pl.pallas_call(functools.partial(dense_kernel, experts), out_shape=(jax.S...  29.1 us
    pallas_call x1, Pallas kernels, dense_shards(): pl.pallas_call(write_kernel, out_shape=tuple((jax.ShapeDtypeStruct(r.shap...  1.07 us

profile of v2, /device:TPU:0, one launch (start us, length us, event | category | flops | bytes accessed | tf_op | source)
XLA Modules:
  0.0 30.8 jit_solution(1414950040690240161)
XLA Ops:
  0.6 29.1 %shard_map.120 = (bf16[32,1024]{1,0:T(8,128)(2,1)S(1)}, bf16[1,256,384]{2,1,0:T(8,128)(2,1)S(1)}, bf16[1,256,384]{2,1,0:T(8,128)(2,1)S(1)}, bf16[1,384,1024]{2,1,0:T(8,128)(2,1)S(1)}) custom-call(bf16[32,1024]{1,0:T(8,128)(2,1)} %tok_hbm.1, bf16[32,1024]{1,0:T(8,128)(2,1)} %cot_hbm.1, s32[8,32]{1,0:T(8,128)} %bitcast.2, bf16[8,32]{1,0:T(8,128)(2,1)} %bitcast.3, ...), custom_call_target="tpu_custom_call" | custom-call | tf_op jit(solution)/shard_map/pallas_call | solution.py:566
  29.8 1.1 %shard_map.121 = (bf16[32,1024]{1,0:T(8,128)(2,1)}, bf16[1,256,384]{2,1,0:T(8,128)(2,1)}, bf16[1,256,384]{2,1,0:T(8,128)(2,1)}, bf16[1,384,1024]{2,1,0:T(8,128)(2,1)}) custom-call(bf16[32,1024]{1,0:T(8,128)(2,1)S(1)} %get-tuple-element.8.refs_0_, bf16[1,256,384]{2,1,0:T(8,128)(2,1)S(1)} %get-tuple-element.9.refs_1_, ...), custom_call_target="tpu_custom_call" | custom-call | tf_op jit(solution)/shard_map/pallas_call | solution.py:612

commit v3 on v2

--- a/solution.py
+++ b/solution.py
@@ -249,14 +249,15 @@
     for j in range(hot_ref.shape[0]):
         limit = limit + jnp.where(expert_row == hot_ref[j], extra_ref[j], 0)
     weights = jnp.where(token_lane < limit, weights, 0.0).astype(bf16)
-    unit = lax.broadcasted_iota(jnp.int32, (names, LANES), 0) == lax.broadcasted_iota(
-        jnp.int32, (names, LANES), 1
-    )
-    weights = lax.dot_general(
-        weights, jnp.where(unit, 1.0, 0.0).astype(bf16), TN, preferred_element_type=f32
-    ).astype(bf16)
-    slab[me, weight_at] = weights[:TILE]
-    slab[me, weight_at + 1] = weights[TILE:]
+    unit_row = lax.broadcasted_iota(jnp.int32, (names, LANES), 0)
+    unit_lane = lax.broadcasted_iota(jnp.int32, (names, LANES), 1)
+
+    def turned(shift):
+        unit = jnp.where(unit_lane == unit_row + shift, 1.0, 0.0).astype(bf16)
+        return lax.dot_general(weights, unit, TN, preferred_element_type=f32)
+
+    main_part, tail_part = turned(0), turned(LANES // 2)
+    slab[me, weight_at] = (main_part[:TILE] + tail_part[TILE:]).astype(bf16)
     tok_tail = tok_ref[TILE:, :].astype(f32)[:8]
     cot_tail = cot_ref[TILE:, :].astype(f32)[:8]
     tail_row = lax.broadcasted_iota(jnp.int32, (8, features), 0)
@@ -272,80 +273,94 @@
 
     pl.semaphore_wait(barrier, 3 + levels - 1)
 
-    def copy_of(s, way, peer):
+    tiles = slab.shape[1]
+    cut = (tiles + 1) // 2
+    pieces = (pl.ds(0, cut), pl.ds(cut, tiles - cut))
+
+    def copy_of(s, p, way, peer):
         return pltpu.make_async_remote_copy(
-            src_ref=slab.at[s],
-            dst_ref=slab.at[s],
-            send_sem=send_sem.at[way, s],
-            recv_sem=recv_sem.at[s],
+            src_ref=slab.at[s, pieces[p]],
+            dst_ref=slab.at[s, pieces[p]],
+            send_sem=send_sem.at[way, p, s],
+            recv_sem=recv_sem.at[p, s],
             device_id=peer,
             device_id_type=MESH,
         )
 
-    def to_x(s):
-        return copy_of(s, 0, to(dx, z, c))
-
-    def to_y(s):
-        return copy_of(s, 1, to(dy, z, c))
-
-    def to_pair(s):
-        return copy_of(s, 2, to(d, z, pc))
-
-    def to_up(s):
-        return copy_of(s, 3, to(d, z + 1, c))
-
-    def to_down(s):
-        return copy_of(s, 4, to(d, z - 1, c))
-
-    def arrived(s):
-        to_pair(s).wait_recv()
-
-    @pl.when(z + 1 < levels)
-    def _():
-        to_up(me).start()
-
-    @pl.when(z > 0)
-    def _():
-        to_down(me).start()
-
-    to_x(me).start()
-    to_y(me).start()
-    to_pair(me).start()
-
+    def to_x(s, p):
+        return copy_of(s, p, 0, to(dx, z, c))
+
+    def to_y(s, p):
+        return copy_of(s, p, 1, to(dy, z, c))
+
+    def to_pair(s, p):
+        return copy_of(s, p, 2, to(d, z, pc))
+
+    def to_level(p, step):
+        return copy_of(me, p, 2 + step, to(d, (z + step) % levels, c))
+
+    def arrived(s, p):
+        to_pair(s, p).wait_recv()
+
+    def at_distance(dist, visit):
+        if dist == 0:
+            visit(z, 0)
+            return
+        pl.when(z - dist >= 0)(lambda: visit(z - dist, -1))
+        pl.when(z + dist < levels)(lambda: visit(z + dist, 1))
+
+    def column(dist, p):
+        def visit(level, side):
+            s = slab_id(d, level, c)
+            if side:
+                arrived(s, p)
+            to_x(s, p).start()
+            to_y(s, p).start()
+            if side == 0:
+                for step in range(1, levels):
+                    to_level(p, step).start()
+            to_pair(s, p).start()
+
+        at_distance(dist, visit)
+
+    def beside(dist, p):
+        def visit(level, side):
+            for dp in (dx, dy):
+                s = slab_id(dp, level, c)
+                arrived(s, p)
+                if p == 0 and dp is dx:
+                    to_y(s, p).start()
+                if p == 1 and dp is dy:
+                    to_x(s, p).start()
+                to_pair(s, p).start()
+
+        at_distance(dist, visit)
+
+    def across(dist):
+        def visit(level, side):
+            s = slab_id(dd, level, c)
+            for p in (0, 1):
+                arrived(s, p)
+                to_pair(s, p).start()
+
+        at_distance(dist, visit)
+
+    def from_pair(dp):
+        for level in range(levels):
+            for p in (0, 1):
+                arrived(slab_id(dp, level, pc), p)
+
+    column(0, 0)
+    column(0, 1)
     for dist in range(1, levels):
-
-        @pl.when(z - dist >= 0)
-        def _():
-            s = slab_id(d, z - dist, c)
-            arrived(s)
-
-            @pl.when(z + 1 < levels)
-            def _():
-                to_up(s).start()
-
-            to_x(s).start()
-            to_y(s).start()
-            to_pair(s).start()
-
-        @pl.when(z + dist < levels)
-        def _():
-            s = slab_id(d, z + dist, c)
-            arrived(s)
-
-            @pl.when(z > 0)
-            def _():
-                to_down(s).start()
-
-            to_x(s).start()
-            to_y(s).start()
-            to_pair(s).start()
-
-    for level in range(levels):
-        arrived(slab_id(d, level, pc))
+        for p in (0, 1):
+            column(dist, p)
+    from_pair(d)
 
     main_rows = experts * TILE
     group_rows = main_rows + experts * 8
-    own_lane = lax.broadcasted_iota(jnp.int32, (group_rows, LANES), 1) == e
+    main_lane = lax.broadcasted_iota(jnp.int32, (main_rows, LANES), 1)
+    tail_lane = lax.broadcasted_iota(jnp.int32, (experts * 8, LANES), 1)
 
     def group(dp, at):
         rows = pl.ds(at, group_rows)
@@ -361,12 +376,15 @@
             hi.append(both[:, 8:].reshape(experts * 8, LANES))
         tail = jnp.concatenate(lo + hi, axis=1)
         cot_rows = pltpu.roll(tail, experts * 8 - 4, 0)
-        w_main = main(weight_at).astype(f32)
-        w_tail = slab[part, weight_at + 1].astype(f32)[:, :8].reshape(experts * 8, LANES)
-        w = jnp.sum(
-            jnp.where(own_lane, jnp.concatenate([w_main, w_tail], axis=0), 0.0),
-            axis=1,
-            keepdims=True,
+        w_all = slab[part, weight_at].astype(f32)
+        w_main = w_all.reshape(main_rows, LANES)
+        w_tail = w_all[:, :8].reshape(experts * 8, LANES)
+        w = jnp.concatenate(
+            [
+                jnp.sum(jnp.where(main_lane == e, w_main, 0.0), axis=1, keepdims=True),
+                jnp.sum(jnp.where(tail_lane == e + LANES // 2, w_tail, 0.0), axis=1, keepdims=True),
+            ],
+            axis=0,
         )
         all_t[rows, :] = jnp.concatenate(
             [jnp.concatenate([main(j) for j in range(blocks)], axis=1), tail.astype(bf16)], axis=0
@@ -419,17 +437,9 @@
     for level in range(levels):
         pair_copy(level).start()
 
-    for level in range(levels):
-        s = slab_id(dx, level, c)
-        arrived(s)
-        if level % 2 == 0:
-            to_y(s).start()
-        to_pair(s).start()
-        s = slab_id(dy, level, c)
-        arrived(s)
-        if level % 2 == 1:
-            to_x(s).start()
-        to_pair(s).start()
+    for dist in range(levels):
+        for p in (0, 1):
+            beside(dist, p)
 
     for level in range(levels):
         pair_copy(level).wait_recv()
@@ -451,16 +461,12 @@
     for step in range(1, levels):
         z_copy(step).start()
 
-    for level in range(levels):
-        arrived(slab_id(dx, level, pc))
+    from_pair(dx)
     group(dx, group_rows)
-    for level in range(levels):
-        s = slab_id(dd, level, c)
-        arrived(s)
-        to_pair(s).start()
-    for level in range(levels):
-        arrived(slab_id(dy, level, pc))
+    from_pair(dy)
     group(dy, 2 * group_rows)
+    for dist in range(levels):
+        across(dist)
     share = features // 4
 
     def weight_terms(at, count):
@@ -474,8 +480,7 @@
 
     early = weight_terms(0, 3 * group_rows)
     acc_gate[...], acc_up[...], acc_down[...] = early
-    for level in range(levels):
-        arrived(slab_id(dd, level, pc))
+    from_pair(dd)
     group(dd, 3 * group_rows)
     late = weight_terms(3 * group_rows, group_rows)
     gg_out[0] = (acc_gate[...] + late[0]).astype(bf16)
@@ -499,28 +504,20 @@
         ).astype(bf16)
 
     for level in range(levels):
+        pair_copy(level).wait_send()
+        to_y(slab_id(dx, level, c), 0).wait_send()
+        to_x(slab_id(dy, level, c), 1).wait_send()
         s = slab_id(d, level, c)
-        to_x(s).wait_send()
-        to_y(s).wait_send()
-        to_pair(s).wait_send()
-        if level % 2 == 0:
-            to_y(slab_id(dx, level, c)).wait_send()
-        else:
-            to_x(slab_id(dy, level, c)).wait_send()
-        for dp in (dx, dy, dd):
-            to_pair(slab_id(dp, level, c)).wait_send()
-        pair_copy(level).wait_send()
-
-        @pl.when((z >= level) & (z + 1 < levels))
-        def _():
-            to_up(s).wait_send()
-
-        @pl.when((z <= level) & (z > 0))
-        def _():
-            to_down(s).wait_send()
+        for p in (0, 1):
+            to_x(s, p).wait_send()
+            to_y(s, p).wait_send()
+            for dp in (d, dx, dy, dd):
+                to_pair(slab_id(dp, level, c), p).wait_send()
 
     for step in range(1, levels):
         z_copy(step).wait_send()
+        to_level(0, step).wait_send()
+        to_level(1, step).wait_send()
 
 
 def write_kernel(*refs):
@@ -542,7 +539,7 @@
     hidden_size = w_gate.shape[2]
     blocks = features // LANES
     levels = experts // 2
-    tiles = 2 * blocks + blocks // 2 + 2
+    tiles = 2 * blocks + blocks // 2 + 1
     back = blocks + blocks // 2
     rows = replicas * experts * (TILE + 8)
     bf16 = jnp.bfloat16
@@ -598,8 +595,8 @@
             pltpu.VMEM((levels, back, TILE, LANES), bf16),
             pltpu.VMEM((levels - 1, back, TILE, LANES), bf16),
             dma((3,)),
-            dma((5, replicas * experts)),
-            dma((replicas * experts,)),
+            dma((levels + 2, 2, replicas * experts)),
+            dma((2, replicas * experts)),
             dma((levels,)),
             dma((levels,)),
             dma((levels - 1,)),

time: 31 us -> 30.1 us (0.971)
  Pallas kernels: 30.2 us -> 29.3 us
    pallas_call x1, Pallas kernels: 29.1 us -> 28.2 us  [dense_shards(): pl.pallas_call(functools.partial(dense_kernel, experts), out_shape=(jax.S...]
where the time goes in v3:
time: 30.1 us; the launch traced here: 29.9 us
  Pallas kernels  29.3 us (97%)
  between operations  0.64 us (2%)
    pallas_call x1, Pallas kernels, dense_shards(): pl.pallas_call(functools.partial(dense_kernel, experts), out_shape=(jax.S...  28.2 us
    pallas_call x1, Pallas kernels, dense_shards(): pl.pallas_call(write_kernel, out_shape=tuple((jax.ShapeDtypeStruct(r.shap...  1.07 us

profile of v3, /device:TPU:0, one launch (start us, length us, event | category | flops | bytes accessed | tf_op | source)
XLA Modules:
  0.0 29.9 jit_solution(2395813359847272964)
XLA Ops:
  0.6 28.2 %shard_map.120 = (bf16[32,1024]{1,0:T(8,128)(2,1)S(1)}, bf16[1,256,384]{2,1,0:T(8,128)(2,1)S(1)}, bf16[1,256,384]{2,1,0:T(8,128)(2,1)S(1)}, bf16[1,384,1024]{2,1,0:T(8,128)(2,1)S(1)}) custom-call(bf16[32,1024]{1,0:T(8,128)(2,1)} %tok_hbm.1, bf16[32,1024]{1,0:T(8,128)(2,1)} %cot_hbm.1, s32[8,32]{1,0:T(8,128)} %bitcast.2, bf16[8,32]{1,0:T(8,128)(2,1)} %bitcast.3, ...), custom_call_target="tpu_custom_call" | custom-call | tf_op jit(solution)/shard_map/pallas_call | solution.py:563
  28.9 1.1 %shard_map.121 = (bf16[32,1024]{1,0:T(8,128)(2,1)}, bf16[1,256,384]{2,1,0:T(8,128)(2,1)}, bf16[1,256,384]{2,1,0:T(8,128)(2,1)}, bf16[1,384,1024]{2,1,0:T(8,128)(2,1)}) custom-call(bf16[32,1024]{1,0:T(8,128)(2,1)S(1)} %get-tuple-element.8.refs_0_, bf16[1,256,384]{2,1,0:T(8,128)(2,1)S(1)} %get-tuple-element.9.refs_1_, ...), custom_call_target="tpu_custom_call" | custom-call | tf_op jit(solution)/shard_map/pallas_call | solution.py:609

commit v4 on v3

--- a/solution.py
+++ b/solution.py
@@ -113,6 +113,7 @@
 MESH = pl.DeviceIdType.MESH
 LANES = 128
 TILE = 16
+WRITE_PARTS = 4
 NT = (((1,), (1,)), ((), ()))
 TN = (((0,), (0,)), ((), ()))
 
@@ -523,9 +524,14 @@
 def write_kernel(*refs):
     sources, sem = refs[: len(refs) // 2], refs[-1]
     targets = refs[len(refs) // 2 : -1]
-    copies = [
-        pltpu.make_async_copy(a, b, sem.at[i]) for i, (a, b) in enumerate(zip(sources, targets))
-    ]
+    copies = []
+    for i, (a, b) in enumerate(zip(sources, targets)):
+        parts = WRITE_PARTS if len(a.shape) == 3 and a.shape[1] % (WRITE_PARTS * TILE) == 0 else 1
+        size = a.shape[-2] // parts
+        for p in range(parts):
+            at = pl.ds(p * size, size)
+            where = (0, at) if len(a.shape) == 3 else (at,)
+            copies.append(pltpu.make_async_copy(a.at[where], b.at[where], sem.at[i, p]))
     for copy in copies:
         copy.start()
     for copy in copies:
@@ -611,7 +617,7 @@
         out_shape=tuple(jax.ShapeDtypeStruct(r.shape, r.dtype) for r in results),
         in_specs=[vmem] * len(results),
         out_specs=tuple(hbm for _ in results),
-        scratch_shapes=[dma((len(results),))],
+        scratch_shapes=[dma((len(results), WRITE_PARTS))],
         compiler_params=pltpu.CompilerParams(vmem_limit_bytes=8 * 1024 * 1024),
     )(*results)
 

time: 30.1 us -> 30.2 us (level)
  no operation moved by 1% of the time
where the time goes in v4:
time: 30.2 us; the launch traced here: 30 us
  Pallas kernels  29.4 us (97%)
  between operations  0.64 us (2%)
    pallas_call x1, Pallas kernels, dense_shards(): pl.pallas_call(functools.partial(dense_kernel, experts), out_shape=(jax.S...  28.2 us
    pallas_call x1, Pallas kernels, dense_shards(): pl.pallas_call(write_kernel, out_shape=tuple((jax.ShapeDtypeStruct(r.shap...  1.16 us

profile of v4, /device:TPU:0, one launch (start us, length us, event | category | flops | bytes accessed | tf_op | source)
XLA Modules:
  0.0 30.0 jit_solution(11277878639705260804)
XLA Ops:
  0.6 28.2 %shard_map.120 = (bf16[32,1024]{1,0:T(8,128)(2,1)S(1)}, bf16[1,256,384]{2,1,0:T(8,128)(2,1)S(1)}, bf16[1,256,384]{2,1,0:T(8,128)(2,1)S(1)}, bf16[1,384,1024]{2,1,0:T(8,128)(2,1)S(1)}) custom-call(bf16[32,1024]{1,0:T(8,128)(2,1)} %tok_hbm.1, bf16[32,1024]{1,0:T(8,128)(2,1)} %cot_hbm.1, s32[8,32]{1,0:T(8,128)} %bitcast.2, bf16[8,32]{1,0:T(8,128)(2,1)} %bitcast.3, ...), custom_call_target="tpu_custom_call" | custom-call | tf_op jit(solution)/shard_map/pallas_call | solution.py:569
  28.9 1.2 %shard_map.121 = (bf16[32,1024]{1,0:T(8,128)(2,1)}, bf16[1,256,384]{2,1,0:T(8,128)(2,1)}, bf16[1,256,384]{2,1,0:T(8,128)(2,1)}, bf16[1,384,1024]{2,1,0:T(8,128)(2,1)}) custom-call(bf16[32,1024]{1,0:T(8,128)(2,1)S(1)} %get-tuple-element.8.refs_0_, bf16[1,256,384]{2,1,0:T(8,128)(2,1)S(1)} %get-tuple-element.9.refs_1_, ...), custom_call_target="tpu_custom_call" | custom-call | tf_op jit(solution)/shard_map/pallas_call | solution.py:615
